TPU v7x, 128 devices: a whole 4x4x4 slice. The times are simulated.
128 devices in a mesh: fsdp: 8 (over x_lo, y), tp: 16 (over z, x_hi, core).
Axes of the slice: x: 4 (x_hi: 2, x_lo: 2; x = x_hi * 2 + x_lo), y: 4, z: 4, core: 2. Of those that a mesh axis runs over, the one named last changes fastest.
Arguments:
- prefix_states: bfloat16 [32768, 8192], P('fsdp', 'tp'), may hold values from -40 to 40
- new_states: bfloat16 [128, 8192], P('fsdp', 'tp'), may hold values from -40 to 40
- w_query: bfloat16 [8192, 8192], P('tp', 'fsdp'), may hold values from -0.09375 to 0.09375
- w_keyvalue: bfloat16 [8192, 2048], P('tp', 'fsdp'), may hold values from -0.03125 to 0.03125
- w_output: bfloat16 [8192, 8192], P('tp', 'fsdp'), may hold values from -0.25 to 0.25
- lengths: int32 [8, 4], P('fsdp'), may hold values from 1 to 1024, 3072 in all within a row
Outputs:
- kv_cache: bfloat16 [32768, 2048], P('fsdp', 'tp')
- mixed: bfloat16 [128, 8192], P('fsdp', 'tp')
Inputs may be any that keep to these rules, and one draw needn't show every extreme that they name: `lengths`: in every group some sequence has length 1024.
All inputs are finite; a program needn't handle non-finite values.
Results may differ from a plain program's by a relative error of at most 0.02.
Values may be sent and summed in bfloat16 or wider, within the bound.
No kernel may reach another device: no remote copies, remote signals or barrier semaphores. Data moves between devices by JAX's collectives and lax.ppermute only.
A program may use at most 128 MiB of HBM per device.

v0:
```python
import jax
import jax.numpy as jnp
from jax import lax
from jax.sharding import PartitionSpec as P

HD = 128
NSEQ = 4
L = 1024
STEPS = 4
theta_base = 500000.0
masked_score = -1e30


def partner(block, axis, apart):
    count = lax.axis_size(axis)
    route = []
    for low in range(count):
        high = low | 1 << apart
        if high != low and high < count:
            route += [(low, high), (high, low)]
    return lax.ppermute(block, axis, route)


def rotate(values, positions):
    half_dim = values.shape[-1] // 2
    frequency = theta_base ** (-2.0 * jnp.arange(half_dim, dtype=jnp.float32) / values.shape[-1])
    angles = positions[:, None, None] * frequency[None, None, :]
    cosine = jnp.cos(angles)
    sine_part = jnp.sin(angles)
    lower_half = values[..., :half_dim]
    upper_half = values[..., half_dim:]
    return jnp.concatenate(
        [
            lower_half * cosine - upper_half * sine_part,
            upper_half * cosine + lower_half * sine_part,
        ],
        axis=-1,
    )


def rotate_columns(column_table, positions):
    half_dim = column_table.shape[0] // 2
    frequency = theta_base ** (
        -2.0 * jnp.arange(half_dim, dtype=jnp.float32) / column_table.shape[0]
    )
    angles = frequency[:, None] * positions[None, :]
    cosine = jnp.cos(angles)
    sine_part = jnp.sin(angles)
    lower_half = column_table[:half_dim]
    upper_half = column_table[half_dim:]
    return jnp.concatenate(
        [
            lower_half * cosine - upper_half * sine_part,
            upper_half * cosine + lower_half * sine_part,
        ],
        axis=0,
    )


def body(prefix_states, new_states, w_query, w_keyvalue, w_output, lengths):
    tp_count = lax.axis_size("tp")
    my_index = lax.axis_index("tp")
    token_count = prefix_states.shape[0]
    fresh_count = new_states.shape[0]
    seq_lengths = lengths[0]
    score_scale = HD ** (-0.5)
    kv_weight = lax.all_gather(w_keyvalue, "fsdp", axis=1, tiled=True)
    kv_width = kv_weight.shape[1]
    query_term = jnp.dot(
        new_states,
        lax.all_gather(w_query, "fsdp", axis=1, tiled=True),
        preferred_element_type=jnp.float32,
    )
    fresh_term = jnp.dot(new_states, kv_weight, preferred_element_type=jnp.float32)
    fresh_positions = (
        jnp.repeat(seq_lengths, STEPS) + jnp.tile(jnp.arange(STEPS, dtype=jnp.int32), NSEQ)
    ).astype(jnp.float32)
    own_rows = kv_width // tp_count
    block_count = own_rows // HD
    block_kind = (my_index * block_count + jnp.arange(block_count, dtype=jnp.int32)) % 2
    cache_sum = lax.psum_scatter(
        lax.dot_general(
            kv_weight, prefix_states, (((0,), (1,)), ((), ())), preferred_element_type=jnp.float32
        ).astype(jnp.bfloat16),
        "tp",
        scatter_dimension=0,
        tiled=True,
    ).astype(jnp.float32)
    slot_positions = (jnp.arange(token_count, dtype=jnp.int32) % L).astype(jnp.float32)
    cache_blocks = cache_sum.reshape(block_count, HD, token_count)
    rotated_blocks = jax.vmap(lambda block_data: rotate_columns(block_data, slot_positions))(
        cache_blocks
    )
    cache_mine = jnp.where((block_kind == 0)[:, None, None], rotated_blocks, cache_blocks).astype(
        jnp.bfloat16
    )
    query_sum, fresh_sum = (
        lax.psum_scatter(query_term, "tp", scatter_dimension=1, tiled=True),
        lax.psum_scatter(fresh_term, "tp", scatter_dimension=1, tiled=True),
    )
    fresh_blocks = fresh_sum.reshape(fresh_count, block_count, HD)
    fresh_rotated = rotate(fresh_blocks, fresh_positions)
    fresh_mine = jnp.where((block_kind == 0)[None, :, None], fresh_rotated, fresh_blocks).astype(
        jnp.bfloat16
    )
    cache_other, fresh_other = partner((cache_mine, fresh_mine), "tp", 0)
    holds_keys = my_index % 2 == 0
    key_table = jnp.where(holds_keys, cache_mine[0], cache_other[0])
    value_table = jnp.where(holds_keys, cache_other[0], cache_mine[0])
    fresh_keys = jnp.where(holds_keys, fresh_mine[:, 0], fresh_other[:, 0])
    fresh_values = jnp.where(holds_keys, fresh_other[:, 0], fresh_mine[:, 0])
    cache_out = cache_mine.reshape(own_rows, token_count).T
    local_heads = query_sum.shape[1] // HD
    query_rot = rotate(query_sum.reshape(fresh_count, local_heads, HD), fresh_positions).astype(
        jnp.bfloat16
    )
    query_four = query_rot.reshape(NSEQ, STEPS, local_heads, HD)
    prefix_scores = (
        jnp.einsum(
            "sjhd,dsl->sjhl",
            query_four,
            key_table.reshape(HD, NSEQ, L),
            preferred_element_type=jnp.float32,
        )
        * score_scale
    )
    live_keys = jnp.arange(L, dtype=jnp.int32)[None, :] < seq_lengths[:, None]
    prefix_scores = jnp.where(live_keys[:, None, None, :], prefix_scores, masked_score)
    fresh_scores = (
        jnp.einsum(
            "sjhd,sid->sjhi",
            query_four,
            fresh_keys.reshape(NSEQ, STEPS, HD),
            preferred_element_type=jnp.float32,
        )
        * score_scale
    )
    causal = jnp.arange(STEPS)[None, :] <= jnp.arange(STEPS)[:, None]
    fresh_scores = jnp.where(causal[None, :, None, :], fresh_scores, masked_score)
    row_max = jnp.maximum(jnp.max(prefix_scores, axis=-1), jnp.max(fresh_scores, axis=-1))
    prefix_weight = jnp.exp(prefix_scores - row_max[..., None])
    fresh_weight = jnp.exp(fresh_scores - row_max[..., None])
    denominator = jnp.sum(prefix_weight, axis=-1) + jnp.sum(fresh_weight, axis=-1)
    numerator = jnp.einsum(
        "sjhl,dsl->sjhd",
        prefix_weight.astype(jnp.bfloat16),
        value_table.reshape(HD, NSEQ, L),
        preferred_element_type=jnp.float32,
    )
    numerator = numerator + jnp.einsum(
        "sjhi,sid->sjhd",
        fresh_weight.astype(jnp.bfloat16),
        fresh_values.reshape(NSEQ, STEPS, HD),
        preferred_element_type=jnp.float32,
    )
    attended = (
        (numerator / denominator[..., None])
        .reshape(fresh_count, local_heads * HD)
        .astype(jnp.bfloat16)
    )
    output_term = jnp.dot(
        attended,
        lax.all_gather(w_output, "fsdp", axis=1, tiled=True),
        preferred_element_type=jnp.float32,
    )
    output_total = lax.psum(output_term, "tp")
    feature_width = output_total.shape[1] // tp_count
    mixed = lax.dynamic_slice_in_dim(output_total, my_index * feature_width, feature_width, 1)
    return (cache_out, mixed.astype(jnp.bfloat16))


def solution(mesh):
    in_specs = (
        P("fsdp", "tp"),
        P("fsdp", "tp"),
        P("tp", "fsdp"),
        P("tp", "fsdp"),
        P("tp", "fsdp"),
        P("fsdp", None),
    )
    out_specs = (P("fsdp", "tp"), P("fsdp", "tp"))
    return jax.shard_map(body, mesh=mesh, in_specs=in_specs, out_specs=out_specs, check_vma=False)
```

profile of v0, /device:TPU:0, one launch (start us, length us, event | category | flops | bytes accessed | tf_op | source)
XLA Modules:
  0.0 613.5 jit_solution(11667397842133907889)
XLA Ops:
  7.2 0.7 all-gather.4.cloned.1.call-update
  8.0 0.7 all-gather.6.cloned.1.call-update
  8.7 48.1 %all-gather.4.cloned.1.call-done = bf16[512,2048]{1,0:T(8,128)(2,1)} async-done(((bf16[512,256]{1,0:T(8,128)(2,1)}), bf16[512,2048]{1,0:T(8,128)(2,1)}) %all-gather.4.cloned.1.call-update) | async-done | bytes 2097168 | tf_op jit(solution)/shard_map/all_gather | solution.py:67
  56.8 14.9 %convolution_convert_fusion = bf16[2048,4096]{1,0:T(8,128)(2,1)} fusion(bf16[512,2048]{1,0:T(8,128)(2,1)} %all-gather.4.cloned.1.call-done, bf16[4096,512]{1,0:T(8,128)(2,1)} %param.6), kind=kOutput, calls=%fused_computation | convolution fusion | flops 8598323200 | bytes 23068672 | tf_op jit(solution)/shard_map/dot_general | solution.py:82
  71.8 1.5 copy-done.2
  73.3 1.0 fusion.57
  74.5 77.4 %all-gather.6.cloned.1.call-done = bf16[512,8192]{1,0:T(8,128)(2,1)} async-done(((bf16[512,1024]{1,0:T(8,128)(2,1)}), bf16[512,8192]{1,0:T(8,128)(2,1)}) %all-gather.6.cloned.1.call-update) | async-done | bytes 8388624 | tf_op jit(solution)/shard_map/all_gather | solution.py:71
  151.8 5.4 fusion.56
  157.3 0.5 all-gather.8.cloned.1.call-update
  158.0 0.1 multiply_cosine_fusion.2
  158.2 144.2 %reduce-scatter.4.cloned.1.call-done = bf16[128,4096]{1,0:T(8,128)(2,1)} async-done(((bf16[2048,4096]{1,0:T(8,128)(2,1)}), bf16[128,4096]{1,0:T(8,128)(2,1)}) %reduce-scatter.4.cloned.1.call-update) | async-done | bytes 1048592 | tf_op jit(solution)/shard_map/reduce_scatter | solution.py:81
  302.3 1.5 convert_bitcast_fusion
  303.8 4.2 fusion.10
  308.1 0.3 fusion
  308.6 56.8 %reduce-scatter.8.cloned.1.call-done = f32[16,128]{1,0:T(8,128)} async-done(((f32[16,2048]{1,0:T(8,128)}), f32[16,128]{1,0:T(8,128)}) %reduce-scatter.8.cloned.1.call-update) | async-done | bytes 8208 | tf_op jit(solution)/shard_map/reduce_scatter | solution.py:99
  365.4 0.9 fusion.44
  366.3 0.1 fusion.47
  366.3 0.2 collective-permute-start.1
  366.6 67.9 %reduce-scatter.6.cloned.1.call-done = f32[16,512]{1,0:T(8,128)} async-done(((f32[16,8192]{1,0:T(8,128)}), f32[16,512]{1,0:T(8,128)}) %reduce-scatter.6.cloned.1.call-update) | async-done | bytes 32784 | tf_op jit(solution)/shard_map/reduce_scatter | solution.py:98
  434.5 0.8 reshape.323
  435.2 0.1 subtract_convert_fusion
  435.3 0.3 fusion.55
  435.7 1.3 copy.13
  437.0 0.8 squeeze.6
  437.8 0.9 fusion.54
  438.7 0.2 fusion.23
  438.9 0.2 fusion.30
  439.1 0.8 fusion.8
  440.0 86.9 %all-gather.8.cloned.1.call-done = bf16[512,8192]{1,0:T(8,128)(2,1)} async-done(((bf16[512,1024]{1,0:T(8,128)(2,1)}), bf16[512,8192]{1,0:T(8,128)(2,1)}) %all-gather.8.cloned.1.call-update) | async-done | bytes 8388624 | tf_op jit(solution)/shard_map/all_gather | solution.py:163
  526.9 4.6 fusion.32
  531.5 74.5 %all-reduce.1 = bf16[16,8192]{1,0:T(8,128)(2,1)S(1)} all-reduce(f32[16,8192]{1,0:T(8,128)S(1)} %fusion.32), channel_id=1, replica_groups=mesh['fsdp'=8,'tp'=16] {'tp'}, use_global_device_ids=true, to_apply=%region_7.8 | all-reduce | flops 131072 | bytes 786432 | tf_op jit(solution)/shard_map/psum | solution.py:166
  606.0 0.6 dynamic-slice_convert_fusion
  (28 shorter events, 0.7 us)
Async XLA Ops:
  7.2 64.7 %copy-start = (bf16[16,512]{1,0:T(8,128)(2,1)S(1)}, bf16[16,512]{1,0:T(8,128)(2,1)}, u32[]{:S(2)}) copy-start(bf16[16,512]{1,0:T(8,128)(2,1)} %param.7) | copy-start | bytes 49156
  7.2 49.7 %all-gather.4.cloned.1.call-start = ((), (), s32[]{:S(2)}) async-start(), calls=%async_computation.3 | async-start | bytes 2359296 | tf_op jit(solution)/shard_map/all_gather | solution.py:67
  7.9 143.9 %all-gather.6.cloned.1.call-start = ((), (), s32[]{:S(2)}) async-start(), calls=%async_computation.5 | async-start | bytes 9437184 | tf_op jit(solution)/shard_map/all_gather | solution.py:71
  8.7 293.6 %reduce-scatter.4.cloned.1.call-start = ((), (), s32[]{:S(2)}) async-start(), calls=%async_computation.4 | async-start | bytes 17825792 | tf_op jit(solution)/shard_map/reduce_scatter | solution.py:81
  71.8 1.6 copy-start.2
  71.8 293.6 %reduce-scatter.8.cloned.1.call-start = ((), (), s32[]{:S(2)}) async-start(), calls=%async_computation.7 | async-start | bytes 139264 | tf_op jit(solution)/shard_map/reduce_scatter | solution.py:99
  74.4 83.4 %copy-start.3 = (s32[1,4]{1,0:T(1,128)S(1)}, s32[1,4]{1,0:T(1,128)}, u32[]{:S(2)}) copy-start(s32[1,4]{1,0:T(1,128)} %param.11) | copy-start | bytes 52
  74.4 360.0 %reduce-scatter.6.cloned.1.call-start = ((), (), s32[]{:S(2)}) async-start(), calls=%async_computation.6 | async-start | bytes 557056 | tf_op jit(solution)/shard_map/reduce_scatter | solution.py:98
  157.2 369.7 %all-gather.8.cloned.1.call-start = ((), (), s32[]{:S(2)}) async-start(), calls=%async_computation.8 | async-start | bytes 9437184 | tf_op jit(solution)/shard_map/all_gather | solution.py:163
  302.3 5.8 copy-start.1
  308.4 128.6 %collective-permute-start = (bf16[1,128,4096]{2,1,0:T(8,128)(2,1)S(1)}, bf16[1,128,4096]{2,1,0:T(8,128)(2,1)S(1)}, u32[]{:S(2)}, u32[]{:S(2)}) collective-permute-start(bf16[1,128,4096]{2,1,0:T(8,128)(2,1)S(1)} %bitcast.69), channel_id=1, source_target_pairs={{0,1},{1,0},{2,3},{3,2},{4,5},{5,4},{6,7},{7,6},{8,9},{9,8},{10,11... | collective-permute-start | bytes 3145736 | tf_op jit(solution)/shard_map/ppermute | solution.py:21
  366.3 69.0 %collective-permute-start.1 = (bf16[16,1,128]{2,0,1:T(8,128)(2,1)S(1)}, bf16[16,1,128]{2,0,1:T(8,128)(2,1)S(1)}, u32[]{:S(2)}, u32[]{:S(2)}) collective-permute-start(bf16[16,1,128]{2,0,1:T(8,128)(2,1)S(1)} %bitcast.79), channel_id=1, source_target_pairs={{0,1},{1,0},{2,3},{3,2},{4,5},{5,4},{6,7},{7,6},{8,9},{9,8},{10,11... | collective-permute-start | bytes 12296 | tf_op jit(solution)/shard_map/ppermute | solution.py:21
Sparse Core Ops, SparseCore 0:
  9.6 47.2 all-gather.3
  58.5 93.3 all-gather.5
  156.2 146.1 reduce-scatter.3
  305.7 59.5 reduce-scatter.7
  369.5 64.9 reduce-scatter.5
  436.0 90.8 all-gather.7
where the time goes:
time: 614 us; the launch traced here: 613 us
  waiting for transfers between devices  483 us (79%)
  blocking collectives  74.5 us (12%)
  matrix products  28.1 us (5%)
  between operations  14.3 us (2%)
  other arithmetic  7.71 us (1%)
    reduce_scatter x1, waiting for transfers between devices, body(): lax.psum_scatter(lax.dot_general(kv_weight, prefix_states, (((0,), (1,)),...  144 us
    all_gather x1, waiting for transfers between devices, body(): lax.all_gather(w_output, 'fsdp', axis=1, tiled=True)  86.9 us
    all_gather x1, waiting for transfers between devices, body(): lax.all_gather(w_query, 'fsdp', axis=1, tiled=True)  77.4 us
    psum x1, blocking collectives, body(): output_total = lax.psum(output_term, 'tp')  74.5 us
    reduce_scatter x1, waiting for transfers between devices, body(): lax.psum_scatter(query_term, 'tp', scatter_dimension=1, tiled=True)  67.9 us
    reduce_scatter x1, waiting for transfers between devices, body(): lax.psum_scatter(fresh_term, 'tp', scatter_dimension=1, tiled=True)  56.8 us
    all_gather x1, waiting for transfers between devices, body(): kv_weight = lax.all_gather(w_keyvalue, 'fsdp', axis=1, tiled=True)  48.1 us
    dot_general x1, matrix products, body(): lax.dot_general(kv_weight, prefix_states, (((0,), (1,)), ((), ())), prefe...  14.9 us
  transfers between devices with their start and end apart: 8, of which 6 were waited for; matrix products, arithmetic and copies ran while one was open for 6% of the time, Pallas kernels for 0%

commit v1 on v0

--- a/solution.py
+++ b/solution.py
@@ -163,7 +163,7 @@
         lax.all_gather(w_output, "fsdp", axis=1, tiled=True),
         preferred_element_type=jnp.float32,
     )
-    output_total = lax.psum(output_term, "tp")
+    output_total = jnp.sum(lax.all_gather(output_term, "tp"), axis=0)
     feature_width = output_total.shape[1] // tp_count
     mixed = lax.dynamic_slice_in_dim(output_total, my_index * feature_width, feature_width, 1)
     return (cache_out, mixed.astype(jnp.bfloat16))

time: 614 us -> 617 us (level)
  blocking collectives: 74.5 us -> 0 us
  waiting for transfers between devices: 483 us -> 555 us
    psum x1 -> x0, blocking collectives: 74.5 us -> none  [body(): output_total = lax.psum(output_term, 'tp')]
    all_gather x0 -> x1, waiting for transfers between devices: none -> 70.4 us  [body(): output_total = jnp.sum(lax.all_gather(output_term, 'tp'), axis=0)]
  transfers between devices with their start and end apart: 8 -> 9, of which waited for: 6 -> 7; matrix products, arithmetic and copies ran while one was open for 6% -> 6% of each run, Pallas kernels for 0% -> 0%
where the time goes in v1:
time: 617 us; the launch traced here: 615 us
  waiting for transfers between devices  555 us (90%)
  matrix products  29 us (5%)
  between operations  14.3 us (2%)
  other arithmetic  11.5 us (2%)
    reduce_scatter x1, waiting for transfers between devices, body(): lax.psum_scatter(lax.dot_general(kv_weight, prefix_states, (((0,), (1,)),...  144 us
    all_gather x1, waiting for transfers between devices, body(): lax.all_gather(w_output, 'fsdp', axis=1, tiled=True)  88.2 us
    all_gather x1, waiting for transfers between devices, body(): lax.all_gather(w_query, 'fsdp', axis=1, tiled=True)  77.4 us
    all_gather x1, waiting for transfers between devices, body(): output_total = jnp.sum(lax.all_gather(output_term, 'tp'), axis=0)  70.4 us
    reduce_scatter x1, waiting for transfers between devices, body(): lax.psum_scatter(query_term, 'tp', scatter_dimension=1, tiled=True)  67.9 us
    reduce_scatter x1, waiting for transfers between devices, body(): lax.psum_scatter(fresh_term, 'tp', scatter_dimension=1, tiled=True)  56.8 us
    all_gather x1, waiting for transfers between devices, body(): kv_weight = lax.all_gather(w_keyvalue, 'fsdp', axis=1, tiled=True)  48.1 us
    dot_general x1, matrix products, body(): lax.dot_general(kv_weight, prefix_states, (((0,), (1,)), ((), ())), prefe...  14.9 us
  transfers between devices with their start and end apart: 9, of which 7 were waited for; matrix products, arithmetic and copies ran while one was open for 6% of the time, Pallas kernels for 0%

profile of v1, /device:TPU:0, one launch (start us, length us, event | category | flops | bytes accessed | tf_op | source)
XLA Modules:
  0.0 615.5 jit_solution(33329522564441813)
XLA Ops:
  7.2 0.7 all-gather.6.cloned.1.call-update
  8.0 0.7 all-gather.8.cloned.1.call-update
  8.7 48.1 %all-gather.6.cloned.1.call-done = bf16[512,2048]{1,0:T(8,128)(2,1)} async-done(((bf16[512,256]{1,0:T(8,128)(2,1)}), bf16[512,2048]{1,0:T(8,128)(2,1)}) %all-gather.6.cloned.1.call-update) | async-done | bytes 2097168 | tf_op jit(solution)/shard_map/all_gather | solution.py:67
  56.8 14.9 %convolution_convert_fusion = bf16[2048,4096]{1,0:T(8,128)(2,1)} fusion(bf16[512,2048]{1,0:T(8,128)(2,1)} %all-gather.6.cloned.1.call-done, bf16[4096,512]{1,0:T(8,128)(2,1)} %param.6), kind=kOutput, calls=%fused_computation | convolution fusion | flops 8598323200 | bytes 23068672 | tf_op jit(solution)/shard_map/dot_general | solution.py:82
  71.8 1.5 copy-done.2
  73.3 1.0 fusion.57
  74.5 77.4 %all-gather.8.cloned.1.call-done = bf16[512,8192]{1,0:T(8,128)(2,1)} async-done(((bf16[512,1024]{1,0:T(8,128)(2,1)}), bf16[512,8192]{1,0:T(8,128)(2,1)}) %all-gather.8.cloned.1.call-update) | async-done | bytes 8388624 | tf_op jit(solution)/shard_map/all_gather | solution.py:71
  151.8 5.4 fusion.56
  157.3 0.5 all-gather.10.cloned.1.call-update
  158.1 0.1 multiply_cosine_fusion.2
  158.2 144.2 %reduce-scatter.4.cloned.1.call-done = bf16[128,4096]{1,0:T(8,128)(2,1)} async-done(((bf16[2048,4096]{1,0:T(8,128)(2,1)}), bf16[128,4096]{1,0:T(8,128)(2,1)}) %reduce-scatter.4.cloned.1.call-update) | async-done | bytes 1048592 | tf_op jit(solution)/shard_map/reduce_scatter | solution.py:81
  302.4 1.5 convert_bitcast_fusion
  303.9 4.2 fusion.10
  308.2 0.3 fusion
  308.7 56.8 %reduce-scatter.8.cloned.1.call-done = f32[16,128]{1,0:T(8,128)} async-done(((f32[16,2048]{1,0:T(8,128)}), f32[16,128]{1,0:T(8,128)}) %reduce-scatter.8.cloned.1.call-update) | async-done | bytes 8208 | tf_op jit(solution)/shard_map/reduce_scatter | solution.py:99
  365.5 0.9 fusion.44
  366.4 0.1 fusion.47
  366.5 0.2 collective-permute-start.1
  366.7 67.9 %reduce-scatter.6.cloned.1.call-done = f32[16,512]{1,0:T(8,128)} async-done(((f32[16,8192]{1,0:T(8,128)}), f32[16,512]{1,0:T(8,128)}) %reduce-scatter.6.cloned.1.call-update) | async-done | bytes 32784 | tf_op jit(solution)/shard_map/reduce_scatter | solution.py:98
  434.6 0.8 reshape.323
  435.4 0.3 fusion.55
  435.8 0.8 squeeze.6
  436.6 0.9 fusion.54
  437.5 0.2 fusion.23
  437.8 0.2 fusion.30
  438.0 0.8 fusion.8
  438.8 88.2 %all-gather.10.cloned.1.call-done = bf16[512,8192]{1,0:T(8,128)(2,1)} async-done(((bf16[512,1024]{1,0:T(8,128)(2,1)}), bf16[512,8192]{1,0:T(8,128)(2,1)}) %all-gather.10.cloned.1.call-update) | async-done | bytes 8388624 | tf_op jit(solution)/shard_map/all_gather | solution.py:163
  527.0 5.4 fusion.32
  532.5 1.3 copy.13
  533.8 70.4 %all-gather.12.cloned.1.call-done = f32[256,8192]{1,0:T(8,128)} async-done(((f32[16,8192]{1,0:T(8,128)}), f32[256,8192]{1,0:T(8,128)}) %all-gather.12.cloned.1.call-update) | async-done | bytes 8388624 | tf_op jit(solution)/shard_map/all_gather | solution.py:166
  604.2 3.8 reduce_sum.29
  608.0 0.6 dynamic-slice_convert_fusion
  (31 shorter events, 0.9 us)
Async XLA Ops:
  7.2 64.7 %copy-start = (bf16[16,512]{1,0:T(8,128)(2,1)S(1)}, bf16[16,512]{1,0:T(8,128)(2,1)}, u32[]{:S(2)}) copy-start(bf16[16,512]{1,0:T(8,128)(2,1)} %param.7) | copy-start | bytes 49156
  7.2 49.7 %all-gather.6.cloned.1.call-start = ((), (), s32[]{:S(2)}) async-start(), calls=%async_computation.3 | async-start | bytes 2359296 | tf_op jit(solution)/shard_map/all_gather | solution.py:67
  7.9 143.9 %all-gather.8.cloned.1.call-start = ((), (), s32[]{:S(2)}) async-start(), calls=%async_computation.5 | async-start | bytes 9437184 | tf_op jit(solution)/shard_map/all_gather | solution.py:71
  8.7 293.7 %reduce-scatter.4.cloned.1.call-start = ((), (), s32[]{:S(2)}) async-start(), calls=%async_computation.4 | async-start | bytes 17825792 | tf_op jit(solution)/shard_map/reduce_scatter | solution.py:81
  71.8 1.6 copy-start.2
  71.8 293.7 %reduce-scatter.8.cloned.1.call-start = ((), (), s32[]{:S(2)}) async-start(), calls=%async_computation.7 | async-start | bytes 139264 | tf_op jit(solution)/shard_map/reduce_scatter | solution.py:99
  74.4 83.5 %copy-start.3 = (s32[1,4]{1,0:T(1,128)S(1)}, s32[1,4]{1,0:T(1,128)}, u32[]{:S(2)}) copy-start(s32[1,4]{1,0:T(1,128)} %param.11) | copy-start | bytes 52
  74.4 360.1 %reduce-scatter.6.cloned.1.call-start = ((), (), s32[]{:S(2)}) async-start(), calls=%async_computation.6 | async-start | bytes 557056 | tf_op jit(solution)/shard_map/reduce_scatter | solution.py:98
  157.2 369.8 %all-gather.10.cloned.1.call-start = ((), (), s32[]{:S(2)}) async-start(), calls=%async_computation.8 | async-start | bytes 9437184 | tf_op jit(solution)/shard_map/all_gather | solution.py:163
  157.8 446.4 %all-gather.12.cloned.1.call-start = ((), (), s32[]{:S(2)}) async-start(), calls=%async_computation.9 | async-start | bytes 8912896 | tf_op jit(solution)/shard_map/all_gather | solution.py:166
  302.4 5.8 copy-start.1
  308.5 127.3 %collective-permute-start = (bf16[1,128,4096]{2,1,0:T(8,128)(2,1)S(1)}, bf16[1,128,4096]{2,1,0:T(8,128)(2,1)S(1)}, u32[]{:S(2)}, u32[]{:S(2)}) collective-permute-start(bf16[1,128,4096]{2,1,0:T(8,128)(2,1)S(1)} %bitcast.71), channel_id=1, source_target_pairs={{0,1},{1,0},{2,3},{3,2},{4,5},{5,4},{6,7},{7,6},{8,9},{9,8},{10,11... | collective-permute-start | bytes 3145736 | tf_op jit(solution)/shard_map/ppermute | solution.py:21
  366.5 69.0 %collective-permute-start.1 = (bf16[16,1,128]{2,0,1:T(8,128)(2,1)S(1)}, bf16[16,1,128]{2,0,1:T(8,128)(2,1)S(1)}, u32[]{:S(2)}, u32[]{:S(2)}) collective-permute-start(bf16[16,1,128]{2,0,1:T(8,128)(2,1)S(1)} %bitcast.81), channel_id=1, source_target_pairs={{0,1},{1,0},{2,3},{3,2},{4,5},{5,4},{6,7},{7,6},{8,9},{9,8},{10,11... | collective-permute-start | bytes 12296 | tf_op jit(solution)/shard_map/ppermute | solution.py:21
Sparse Core Ops, SparseCore 0:
  9.6 47.2 all-gather.5
  58.5 93.3 all-gather.7
  156.2 146.1 reduce-scatter.3
  305.8 59.6 reduce-scatter.7
  369.6 64.9 reduce-scatter.5
  436.1 90.8 all-gather.9
  532.6 71.5 all-gather.11
